TPU v7x, 32 devices: a whole 2x2x4 slice. The times are simulated.
32 devices in a mesh: wide: 8 (over z, y), narrow: 4 (over x, core).
Axes of the slice: x: 2, y: 2, z: 4, core: 2. Of those that a mesh axis runs over, the one named last changes fastest.
Arguments:
- probes: bfloat16 [32768, 256], P(('wide', 'narrow')), may hold values from -6 to 6
- leaf_basis: bfloat16 [64, 512, 256], P(('wide', 'narrow')), may hold values from -0.25 to 0.25
- transfer: bfloat16 [5, 2, 256, 256], replicated, may hold values from -0.375 to 0.375
- coupling_pool: bfloat16 [6, 3, 256, 256], replicated, may hold values from -0.375 to 0.375
- coupling_ids: int32 [126], replicated, may hold values from 0 to 2
- near_blocks: bfloat16 [64, 3, 512, 512], P(('wide', 'narrow')), may hold values from -0.25 to 0.25
- near_mask: int32 [64, 2], P(('wide', 'narrow')), may hold values 0 or 1
Outputs:
- product: bfloat16 [32768, 256], P(('wide', 'narrow'))
Inputs may be any that keep to these rules, and one draw needn't show every extreme that they name: `coupling_ids`: entry 2 * 64 - 2 (64 / 2^l) + a gives the coupling block of node a of level l. `near_mask`: column 0 is the left neighbour, column 1 the right one.
All inputs are finite; a program needn't handle non-finite values. No bound on the sum of `near_mask` on one device may be relied on, other than what follows from the above.
Results may differ from a plain program's by a relative error of at most 0.018.
Values may be sent and summed in bfloat16 or wider, within the bound.
A program may use at most 64 MiB of HBM per device.

v0:
```python
import jax
import jax.numpy as jnp
from jax import lax
from jax.sharding import PartitionSpec as P

LEAF = 512


half_root = 0.7071067811865476


def from_partner(value, axis, stride):
    return lax.ppermute(value, axis, [(i, i ^ 1 << stride) for i in range(lax.axis_size(axis))])


def extended_2(block, sides, width):
    for axis, dim in sides:
        count = lax.axis_size(axis)
        forward = [(i, i + 1) for i in range(count - 1)]
        backward = [(target, source) for source, target in forward]
        low = lax.ppermute(
            lax.slice_in_dim(block, block.shape[dim] - width, None, axis=dim), axis, forward
        )
        high = lax.ppermute(lax.slice_in_dim(block, 0, width, axis=dim), axis, backward)
        block = jnp.concatenate([low, block, high], axis=dim)
    return block


def lift_pairs(block, trans_level):
    count, rank, width = block.shape
    pairs = block.reshape(count // 2, 2, rank, width)
    left = jnp.einsum(
        "sr,ksp->krp", trans_level[0], pairs[:, 0], preferred_element_type=jnp.float32
    )
    right = jnp.einsum(
        "sr,ksp->krp", trans_level[1], pairs[:, 1], preferred_element_type=jnp.float32
    )
    return ((left + right) * half_root).astype(jnp.bfloat16)


def order_pair(own, other, parity):
    first = jnp.where(parity == 0, own, other)
    second = jnp.where(parity == 0, other, own)
    return jnp.concatenate([first, second], axis=0)


def couple(pool_level, coupling_ids, block, base, offset):
    count, rank, width = block.shape
    sibling = block.reshape(count // 2, 2, rank, width)[:, ::-1].reshape(count, rank, width)
    picks = lax.dynamic_slice_in_dim(coupling_ids, offset + base, count)
    mats = jnp.take(pool_level, picks, axis=0)
    return jnp.einsum("krs,ksp->krp", mats, sibling, preferred_element_type=jnp.float32)


def on_device(probes, leaf_basis, transfer, coupling_pool, coupling_ids, near_blocks, near_mask):
    leaf_dev, leaf_rows, rank = leaf_basis.shape
    width = probes.shape[1]
    n_narrow = lax.axis_size("narrow")
    n_wide = lax.axis_size("wide")
    narrow_bits = n_narrow.bit_length() - 1
    wide_bits = n_wide.bit_length() - 1
    local_bits = leaf_dev.bit_length() - 1
    levels = local_bits + narrow_bits + wide_bits
    leaves = leaf_dev * n_narrow * n_wide
    device = lax.axis_index(("wide", "narrow"))
    first_leaf = device * leaf_dev
    panels = probes.reshape(leaf_dev, leaf_rows, width)
    block = jnp.einsum(
        "kir,kip->krp", leaf_basis, panels, preferred_element_type=jnp.float32
    ).astype(jnp.bfloat16)
    base = first_leaf
    blocks = []
    bases = []
    lifted = []
    for level in range(levels):
        own_node = first_leaf >> level
        if block.shape[0] == 1:
            lifted.append(False)
            if level - local_bits < narrow_bits:
                other = from_partner(block, "narrow", level - local_bits)
                parity = own_node & 1
                block = order_pair(block, other, parity)
                base = own_node - parity
            else:
                other = from_partner(block, "wide", level - local_bits - narrow_bits)
                parity = own_node & 1
                block = order_pair(block, other, parity)
                base = own_node - parity
        else:
            lifted.append(level > 0)
        blocks.append(block)
        bases.append(base)
        if level < levels - 1:
            block = lift_pairs(block, transfer[level])
            base = base >> 1

    def offset_of(level):
        return 2 * leaves - 2 * (leaves >> level)

    top = levels - 1
    field = couple(coupling_pool[top], coupling_ids, blocks[top], bases[top], offset_of(top))
    for level in range(levels - 2, -1, -1):
        coarse = field.astype(jnp.bfloat16)
        position = (first_leaf >> level + 1) - bases[level + 1]
        coarse = lax.dynamic_index_in_dim(coarse, position, 0, keepdims=True)
        even = jnp.einsum(
            "rs,ksp->krp", transfer[level, 0], coarse, preferred_element_type=jnp.float32
        )
        odd = jnp.einsum(
            "rs,ksp->krp", transfer[level, 1], coarse, preferred_element_type=jnp.float32
        )
        spread = jnp.stack([even, odd], axis=1).reshape(-1, rank, width)
        field = (
            couple(
                coupling_pool[level], coupling_ids, blocks[level], bases[level], offset_of(level)
            )
            + spread
        )
    far = jnp.einsum(
        "kir,krp->kip", leaf_basis, field.astype(jnp.bfloat16), preferred_element_type=jnp.float32
    )
    extended = extended_2(probes, ((("wide", "narrow"), 0),), LEAF)
    stacked = extended.reshape(leaf_dev + 2, leaf_rows, width)
    weights = near_mask.astype(jnp.float32)
    before = jnp.einsum(
        "kij,kjp->kip", near_blocks[:, 0], stacked[:-2], preferred_element_type=jnp.float32
    )
    middle = jnp.einsum(
        "kij,kjp->kip", near_blocks[:, 1], stacked[1:-1], preferred_element_type=jnp.float32
    )
    after = jnp.einsum(
        "kij,kjp->kip", near_blocks[:, 2], stacked[2:], preferred_element_type=jnp.float32
    )
    total = far + before * weights[:, 0, None, None] + middle + after * weights[:, 1, None, None]
    return total.astype(jnp.bfloat16).reshape(leaf_dev * leaf_rows, width)


def solution(mesh):
    in_specs = (
        P(("wide", "narrow"), None),
        P(("wide", "narrow"), None, None),
        P(),
        P(),
        P(),
        P(("wide", "narrow"), None, None, None),
        P(("wide", "narrow"), None),
    )
    out_specs = P(("wide", "narrow"), None)
    return jax.shard_map(
        on_device, mesh=mesh, in_specs=in_specs, out_specs=out_specs, check_vma=False
    )
```

profile of v0, /device:TPU:0, one launch (start us, length us, event | category | flops | bytes accessed | tf_op | source)
XLA Modules:
  0.0 62.1 jit_solution(6518212416438154147)
XLA Ops:
  0.0 1.4 %copy-done = bf16[2,512,256]{2,1,0:T(8,128)(2,1)S(1)} copy-done((bf16[2,512,256]{2,1,0:T(8,128)(2,1)S(1)}, bf16[2,512,256]{2,1,0:T(8,128)(2,1)}, u32[]{:S(2)}) %copy-start) | copy-done | bytes 524312
  1.4 1.4 %convolution_convert_fusion = bf16[2,256,256]{2,1,0:T(8,128)(2,1)S(1)} fusion(bf16[2,512,256]{2,1,0:T(8,128)(2,1)S(1)} %copy-done, bf16[2,512,256]{2,1,0:T(8,128)(2,1)} %bitcast.248), kind=kOutput, calls=%fused_computation.16 | convolution fusion | flops 134348800 | bytes 1310720 | tf_op jit(solution)/shard_map/kir,kip->krp/dot_general | solution.py:68
  2.9 1.2 %fusion.64 = f32[256,256]{1,0:T(8,128)S(1)} fusion(bf16[1,2,256,256]{3,2,1,0:T(8,128)(2,1)S(1)} %bitcast.252, bf16[5,2,256,256]{3,2,1,0:T(8,128)(2,1)} %param.11), kind=kOutput, calls=%fused_computation.122 | convolution fusion | flops 33554432 | bytes 524288 | tf_op jit(solution)/shard_map/sr,ksp->krp/dot_general | solution.py:32
  4.1 0.9 %fusion.20 = bf16[1,256,256]{1,2,0:T(8,128)(2,1)} fusion(f32[256,256]{1,0:T(8,128)S(1)} %fusion.64, bf16[1,2,256,256]{3,2,1,0:T(8,128)(2,1)S(1)} %bitcast.253, bf16[5,2,256,256]{3,2,1,0:T(8,128)(2,1)S(1)} %copy-done.2), kind=kOutput, calls=%fused_computation.46 | convolution fusion | flops 33751040 | bytes 655360 | tf_op jit(solution)/shard_map/sr,ksp->krp/dot_general | solution.py:35
  5.5 0.8 %fusion.126 = (bf16[512,256]{1,0:T(8,128)(2,1)}, bf16[512,256]{1,0:T(8,128)(2,1)}) fusion(bf16[1024,256]{1,0:T(8,128)(2,1)S(1)} %copy-done.1), kind=kLoop, calls=%fused_computation.212 | loop fusion | bytes 1048576 | tf_op jit(solution)/shard_map/slice | solution.py:24
  6.3 2.6 %collective-permute-start.5 = (bf16[512,256]{1,0:T(8,128)(2,1)}, bf16[512,256]{1,0:T(8,128)(2,1)}, u32[]{:S(2)}, u32[]{:S(2)}) collective-permute-start(bf16[512,256]{1,0:T(8,128)(2,1)} %get-tuple-element.29), channel_id=1, source_target_pairs={{0,1},{1,2},{2,3},{3,4},{4,5},{5,6},{6,7},{7,8},{8,9},{9,10},{10,1... | collective-permute-start | bytes 786440 | tf_op jit(solution)/shard_map/ppermute | solution.py:21
  8.9 1.3 %collective-permute-start.6 = (bf16[512,256]{1,0:T(8,128)(2,1)}, bf16[512,256]{1,0:T(8,128)(2,1)}, u32[]{:S(2)}, u32[]{:S(2)}) collective-permute-start(bf16[512,256]{1,0:T(8,128)(2,1)} %get-tuple-element.28), channel_id=1, source_target_pairs={{1,0},{2,1},{3,2},{4,3},{5,4},{6,5},{7,6},{8,7},{9,8},{10,9},{11,1... | collective-permute-start | bytes 786440 | tf_op jit(solution)/shard_map/ppermute | solution.py:24
  10.2 0.7 %compare_and_fusion.5 = (pred[2]{0:T(512)(128)(4,1)}, s32[2]{0:T(128)S(1)}, pred[2]{0:T(512)(128)(4,1)}, s32[2]{0:T(128)S(1)}, pred[2]{0:T(512)(128)(4,1)}, /*in...) fusion(s32[126]{0:T(128)S(1)} %copy-done.10, ...), kind=kLoop, calls=%fused_computation.198 | loop fusion | flops 72 | bytes 132 | tf_op jit(solution)/shard_map/jit(_take)/and | solution.py:51
  10.9 0.6 pad_clamp_fusion.1
  11.5 2.7 %slice_bitcast_fusion.5 = (bf16[3,256,256]{2,1,0:T(8,128)(2,1)S(1)}, bf16[3,256,256]{2,1,0:T(8,128)(2,1)}, bf16[3,256,256]{2,1,0:T(8,128)(2,1)S(1)}, bf16[3,256,...) fusion(bf16[6,3,256,256]{3,2,1,0:T(8,128)(2,1)} %param.12), kind=kLoop, calls=%fused_computation.65 | loop fusion | bytes 4718592 | tf_op jit(solution)/shard_map/squeeze | solution.py:115
  14.2 0.6 pad_clamp_fusion
  14.8 0.6 pad_clamp_fusion.2
  15.4 0.7 %convert_element_type.94 = f32[2,2]{1,0:T(2,128)S(1)} convert(s32[2,2]{1,0:T(2,128)} %param.15) | non-fusion elementwise | flops 4 | bytes 32 | tf_op jit(solution)/shard_map/convert_element_type | solution.py:124
  16.1 2.4 %gather_fusion.4 = bf16[2,256,256]{2,1,0:T(8,128)(2,1)} fusion(bf16[3,256,256]{2,1,0:T(8,128)(2,1)} %get-tuple-element.25, s32[1024]{0:T(1024)} %pad_clamp_fusion.1), kind=kCustom, calls=%fused_computation.4.clone | custom fusion | bytes 524296 | tf_op jit(solution)/shard_map/jit(_take)/gather | solution.py:51
  18.5 2.4 %gather_fusion.5 = bf16[2,256,256]{2,1,0:T(8,128)(2,1)} fusion(bf16[3,256,256]{2,1,0:T(8,128)(2,1)} %get-tuple-element.24, s32[1024]{0:T(1024)} %pad_clamp_fusion), kind=kCustom, calls=%fused_computation.5.clone | custom fusion | bytes 524296 | tf_op jit(solution)/shard_map/jit(_take)/gather | solution.py:51
  20.9 2.4 %gather_fusion.3 = bf16[2,256,256]{2,1,0:T(8,128)(2,1)} fusion(bf16[3,256,256]{2,1,0:T(8,128)(2,1)} %get-tuple-element.21, s32[1024]{0:T(1024)} %pad_clamp_fusion.2), kind=kCustom, calls=%fused_computation.3.clone | custom fusion | bytes 524296 | tf_op jit(solution)/shard_map/jit(_take)/gather | solution.py:51
  23.3 1.3 %gather_fusion.2 = bf16[2,256,256]{2,1,0:T(8,128)(2,1)} fusion(bf16[3,256,256]{2,1,0:T(8,128)(2,1)S(1)} %get-tuple-element.22, s32[1024]{0:T(1024)S(1)} %pad_clamp_fusion.3), kind=kCustom, calls=%fused_computation.2.clone | custom fusion | bytes 524296 | tf_op jit(solution)/shard_map/jit(_take)/gather | solution.py:51
  24.5 0.6 gather_fusion.1
  25.1 0.6 gather_fusion
  25.9 1.0 %broadcast_select_fusion.9 = (bf16[1,256,256]{1,2,0:T(8,128)(2,1)S(1)}, bf16[1,256,256]{1,2,0:T(8,128)(2,1)S(1)}) fusion(bf16[1,256,256]{1,2,0:T(8,128)(2,1)} %fusion.20, bf16[1,256,256]{1,2,0:T(8,128)(2,1)} %collective-permute-done, pred[]{:T(512)S(6)} %eq.20), kind=kLoop, calls=%fused_computation.158 | loop fusion | flops 131072 | bytes 524289 | tf_op jit(solution)/shard_map/jit(_where)/select_n | solution.py:42
  27.3 4.2 %collective-permute-start.1 = (bf16[1,256,256]{1,2,0:T(8,128)(2,1)S(1)}, bf16[1,256,256]{1,2,0:T(8,128)(2,1)S(1)}, u32[]{:S(2)}, u32[]{:S(2)}) collective-permute-start(bf16[1,256,256]{1,2,0:T(8,128)(2,1)S(1)} %fusion.19), channel_id=1, source_target_pairs={{0,2},{1,3},{2,0},{3,1},{4,6},{5,7},{6,4},{7,5},{8,10},{9,11},{10,... | collective-permute-start | bytes 393224 | tf_op jit(solution)/shard_map/ppermute | solution.py:13
  31.8 3.5 %collective-permute-done.1 = bf16[1,256,256]{1,2,0:T(8,128)(2,1)S(1)} collective-permute-done((bf16[1,256,256]{1,2,0:T(8,128)(2,1)S(1)}, bf16[1,256,256]{1,2,0:T(8,128)(2,1)S(1)}, u32[]{:S(2)}, u32[]{:S(2)}) %collective-permute-start.1) | collective-permute-done | bytes 131104 | tf_op jit(solution)/shard_map/ppermute | solution.py:13
  35.7 2.2 %collective-permute-start.2 = (bf16[1,256,256]{1,2,0:T(8,128)(2,1)S(1)}, bf16[1,256,256]{1,2,0:T(8,128)(2,1)S(1)}, u32[]{:S(2)}, u32[]{:S(2)}) collective-permute-start(bf16[1,256,256]{1,2,0:T(8,128)(2,1)S(1)} %fusion.18), channel_id=1, source_target_pairs={{0,4},{4,0},{8,12},{12,8},{16,20},{20,16},{24,28},{28,24},{1,5},{5... | collective-permute-start | bytes 393224 | tf_op jit(solution)/shard_map/ppermute | solution.py:13
  38.2 1.1 %pad_maximum_fusion = (bf16[1024,256]{1,0:T(8,128)(2,1)S(1)}, bf16[1024,256]{1,0:T(8,128)(2,1)S(1)}) fusion(bf16[512,256]{1,0:T(8,128)(2,1)} %collective-permute-done.6, bf16[1024,256]{1,0:T(8,128)(2,1)S(1)} %copy-done.1, bf16[512,256]{1,0:T(8,128)(2,1)} %collective-permute-done.5), kind=kLoop, calls=%fused_computation.53 | loop fusion | flops 2097152 | bytes 2097152 | tf_op jit(solution)/shard_map/concatenate | solution.py:25
  39.3 1.5 %collective-permute-done.2 = bf16[1,256,256]{1,2,0:T(8,128)(2,1)S(1)} collective-permute-done((bf16[1,256,256]{1,2,0:T(8,128)(2,1)S(1)}, bf16[1,256,256]{1,2,0:T(8,128)(2,1)S(1)}, u32[]{:S(2)}, u32[]{:S(2)}) %collective-permute-start.2) | collective-permute-done | bytes 131104 | tf_op jit(solution)/shard_map/ppermute | solution.py:13
  41.3 3.0 %collective-permute-start.3 = (bf16[1,256,256]{1,2,0:T(8,128)(2,1)S(1)}, bf16[1,256,256]{1,2,0:T(8,128)(2,1)S(1)}, u32[]{:S(2)}, u32[]{:S(2)}) collective-permute-start(bf16[1,256,256]{1,2,0:T(8,128)(2,1)S(1)} %fusion.17), channel_id=1, source_target_pairs={{0,8},{4,12},{8,0},{12,4},{16,24},{20,28},{24,16},{28,20},{1,9},{5... | collective-permute-start | bytes 393224 | tf_op jit(solution)/shard_map/ppermute | solution.py:13
  44.7 3.4 %collective-permute-done.3 = bf16[1,256,256]{1,2,0:T(8,128)(2,1)S(1)} collective-permute-done((bf16[1,256,256]{1,2,0:T(8,128)(2,1)S(1)}, bf16[1,256,256]{1,2,0:T(8,128)(2,1)S(1)}, u32[]{:S(2)}, u32[]{:S(2)}) %collective-permute-start.3) | collective-permute-done | bytes 131104 | tf_op jit(solution)/shard_map/ppermute | solution.py:13
  48.5 2.8 %collective-permute-start.4 = (bf16[1,256,256]{1,2,0:T(8,128)(2,1)S(1)}, bf16[1,256,256]{1,2,0:T(8,128)(2,1)S(1)}, u32[]{:S(2)}, u32[]{:S(2)}) collective-permute-start(bf16[1,256,256]{1,2,0:T(8,128)(2,1)S(1)} %fusion.16), channel_id=1, source_target_pairs={{0,16},{4,20},{8,24},{12,28},{16,0},{20,4},{24,8},{28,12},{1,17},{... | collective-permute-start | bytes 393224 | tf_op jit(solution)/shard_map/ppermute | solution.py:13
  51.6 2.9 %collective-permute-done.4 = bf16[1,256,256]{1,2,0:T(8,128)(2,1)S(1)} collective-permute-done((bf16[1,256,256]{1,2,0:T(8,128)(2,1)S(1)}, bf16[1,256,256]{1,2,0:T(8,128)(2,1)S(1)}, u32[]{:S(2)}, u32[]{:S(2)}) %collective-permute-start.4) | collective-permute-done | bytes 131104 | tf_op jit(solution)/shard_map/ppermute | solution.py:13
  58.2 1.2 %copy-done.3 = bf16[2,3,512,512]{3,2,1,0:T(8,128)(2,1)S(1)} copy-done((bf16[2,3,512,512]{3,2,1,0:T(8,128)(2,1)S(1)}, bf16[2,3,512,512]{3,2,1,0:T(8,128)(2,1)}, u32[]{:S(2)}) %copy-start.3) | copy-done | bytes 3145752
  59.5 0.5 fusion.3
  61.1 1.0 %copy.46 = bf16[2,512,256]{2,1,0:T(8,128)(2,1)} copy(bf16[2,512,256]{1,2,0:T(8,128)(2,1)S(1)} %fusion.4) | data formatting | bytes 1048576 | tf_op jit(solution)/shard_map/convert_element_type | solution.py:135
  (83 shorter events, 8.1 us)
Async XLA Ops:
  0.0 1.4 %copy-start = (bf16[2,512,256]{2,1,0:T(8,128)(2,1)S(1)}, bf16[2,512,256]{2,1,0:T(8,128)(2,1)}, u32[]{:S(2)}) copy-start(bf16[2,512,256]{2,1,0:T(8,128)(2,1)} %param.10) | copy-start | bytes 1572868
  0.0 5.5 %copy-start.1 = (bf16[1024,256]{1,0:T(8,128)(2,1)S(1)}, bf16[1024,256]{1,0:T(8,128)(2,1)}, u32[]{:S(2)}) copy-start(bf16[1024,256]{1,0:T(8,128)(2,1)} %param.9) | copy-start | bytes 1572868
  0.0 4.1 %copy-start.2 = (bf16[5,2,256,256]{3,2,1,0:T(8,128)(2,1)S(1)}, bf16[5,2,256,256]{3,2,1,0:T(8,128)(2,1)}, u32[]{:S(2)}) copy-start(bf16[5,2,256,256]{3,2,1,0:T(8,128)(2,1)} %param.11) | copy-start | bytes 3932164
  2.8 1.3 %copy-start.4 = (bf16[2,256,256]{2,1,0:T(8,128)(2,1)}, bf16[2,256,256]{2,1,0:T(8,128)(2,1)S(1)}, u32[]{:S(2)}) copy-start(bf16[2,256,256]{2,1,0:T(8,128)(2,1)S(1)} %convolution_convert_fusion) | copy-start | bytes 786436
  2.8 7.4 %copy-start.10 = (s32[126]{0:T(128)S(1)}, s32[126]{0:T(128)}, u32[]{:S(2)}) copy-start(s32[126]{0:T(128)} %param.13) | copy-start | bytes 1516
  5.0 20.9 %collective-permute-start = (bf16[1,256,256]{1,2,0:T(8,128)(2,1)}, bf16[1,256,256]{1,2,0:T(8,128)(2,1)}, u32[]{:S(2)}, u32[]{:S(2)}) collective-permute-start(bf16[1,256,256]{1,2,0:T(8,128)(2,1)} %fusion.20), channel_id=1, source_target_pairs={{0,1},{1,0},{2,3},{3,2},{4,5},{5,4},{6,7},{7,6},{8,9},{9,8},{10,11... | collective-permute-start | bytes 393224 | tf_op jit(solution)/shard_map/ppermute | solution.py:13
  6.3 31.9 %collective-permute-start.5 = (bf16[512,256]{1,0:T(8,128)(2,1)}, bf16[512,256]{1,0:T(8,128)(2,1)}, u32[]{:S(2)}, u32[]{:S(2)}) collective-permute-start(bf16[512,256]{1,0:T(8,128)(2,1)} %get-tuple-element.29), channel_id=1, source_target_pairs={{0,1},{1,2},{2,3},{3,4},{4,5},{5,6},{6,7},{7,8},{8,9},{9,10},{10,1... | collective-permute-start | bytes 786440 | tf_op jit(solution)/shard_map/ppermute | solution.py:21
  8.9 29.3 %collective-permute-start.6 = (bf16[512,256]{1,0:T(8,128)(2,1)}, bf16[512,256]{1,0:T(8,128)(2,1)}, u32[]{:S(2)}, u32[]{:S(2)}) collective-permute-start(bf16[512,256]{1,0:T(8,128)(2,1)} %get-tuple-element.28), channel_id=1, source_target_pairs={{1,0},{2,1},{3,2},{4,3},{5,4},{6,5},{7,6},{8,7},{9,8},{10,9},{11,1... | collective-permute-start | bytes 786440 | tf_op jit(solution)/shard_map/ppermute | solution.py:24
  25.1 6.4 %copy-start.16 = (pred[2]{0:T(512)(128)(4,1)S(1)}, pred[2]{0:T(512)(128)(4,1)}, u32[]{:S(2)}) copy-start(pred[2]{0:T(512)(128)(4,1)} %get-tuple-element.44) | copy-start | bytes 10
  27.3 8.0 %collective-permute-start.1 = (bf16[1,256,256]{1,2,0:T(8,128)(2,1)S(1)}, bf16[1,256,256]{1,2,0:T(8,128)(2,1)S(1)}, u32[]{:S(2)}, u32[]{:S(2)}) collective-permute-start(bf16[1,256,256]{1,2,0:T(8,128)(2,1)S(1)} %fusion.19), channel_id=1, source_target_pairs={{0,2},{1,3},{2,0},{3,1},{4,6},{5,7},{6,4},{7,5},{8,10},{9,11},{10,... | collective-permute-start | bytes 393224 | tf_op jit(solution)/shard_map/ppermute | solution.py:13
  31.8 6.1 %copy-start.9 = (bf16[2,256,256]{2,1,0:T(8,128)(2,1)S(1)}, bf16[2,256,256]{2,1,0:T(8,128)(2,1)}, u32[]{:S(2)}) copy-start(bf16[2,256,256]{2,1,0:T(8,128)(2,1)} %gather_fusion.2) | copy-start | bytes 786436
  31.8 6.1 %copy-start.15 = (pred[2]{0:T(512)(128)(4,1)S(1)}, pred[2]{0:T(512)(128)(4,1)}, u32[]{:S(2)}) copy-start(pred[2]{0:T(512)(128)(4,1)} %get-tuple-element.42) | copy-start | bytes 10
  35.7 5.1 %collective-permute-start.2 = (bf16[1,256,256]{1,2,0:T(8,128)(2,1)S(1)}, bf16[1,256,256]{1,2,0:T(8,128)(2,1)S(1)}, u32[]{:S(2)}, u32[]{:S(2)}) collective-permute-start(bf16[1,256,256]{1,2,0:T(8,128)(2,1)S(1)} %fusion.18), channel_id=1, source_target_pairs={{0,4},{4,0},{8,12},{12,8},{16,20},{20,16},{24,28},{28,24},{1,5},{5... | collective-permute-start | bytes 393224 | tf_op jit(solution)/shard_map/ppermute | solution.py:13
  39.3 5.0 %copy-start.8 = (bf16[2,256,256]{2,1,0:T(8,128)(2,1)S(1)}, bf16[2,256,256]{2,1,0:T(8,128)(2,1)}, u32[]{:S(2)}) copy-start(bf16[2,256,256]{2,1,0:T(8,128)(2,1)} %gather_fusion.3) | copy-start | bytes 786436
  39.3 5.0 %copy-start.14 = (pred[2]{0:T(512)(128)(4,1)S(1)}, pred[2]{0:T(512)(128)(4,1)}, u32[]{:S(2)}) copy-start(pred[2]{0:T(512)(128)(4,1)} %get-tuple-element.40) | copy-start | bytes 10
  41.3 6.7 %collective-permute-start.3 = (bf16[1,256,256]{1,2,0:T(8,128)(2,1)S(1)}, bf16[1,256,256]{1,2,0:T(8,128)(2,1)S(1)}, u32[]{:S(2)}, u32[]{:S(2)}) collective-permute-start(bf16[1,256,256]{1,2,0:T(8,128)(2,1)S(1)} %fusion.17), channel_id=1, source_target_pairs={{0,8},{4,12},{8,0},{12,4},{16,24},{20,28},{24,16},{28,20},{1,9},{5... | collective-permute-start | bytes 393224 | tf_op jit(solution)/shard_map/ppermute | solution.py:13
  44.6 6.7 %copy-start.7 = (bf16[2,256,256]{2,1,0:T(8,128)(2,1)S(1)}, bf16[2,256,256]{2,1,0:T(8,128)(2,1)}, u32[]{:S(2)}) copy-start(bf16[2,256,256]{2,1,0:T(8,128)(2,1)} %gather_fusion.4) | copy-start | bytes 786436
  44.6 6.7 %copy-start.13 = (pred[2]{0:T(512)(128)(4,1)S(1)}, pred[2]{0:T(512)(128)(4,1)}, u32[]{:S(2)}) copy-start(pred[2]{0:T(512)(128)(4,1)} %get-tuple-element.48) | copy-start | bytes 10
  48.1 6.4 %copy-start.6 = (bf16[2,256,256]{2,1,0:T(8,128)(2,1)S(1)}, bf16[2,256,256]{2,1,0:T(8,128)(2,1)}, u32[]{:S(2)}) copy-start(bf16[2,256,256]{2,1,0:T(8,128)(2,1)} %gather_fusion.5) | copy-start | bytes 786436
  48.1 6.4 %copy-start.12 = (pred[2]{0:T(512)(128)(4,1)S(1)}, pred[2]{0:T(512)(128)(4,1)}, u32[]{:S(2)}) copy-start(pred[2]{0:T(512)(128)(4,1)} %get-tuple-element.46) | copy-start | bytes 10
  48.5 5.9 %collective-permute-start.4 = (bf16[1,256,256]{1,2,0:T(8,128)(2,1)S(1)}, bf16[1,256,256]{1,2,0:T(8,128)(2,1)S(1)}, u32[]{:S(2)}, u32[]{:S(2)}) collective-permute-start(bf16[1,256,256]{1,2,0:T(8,128)(2,1)S(1)} %fusion.16), channel_id=1, source_target_pairs={{0,16},{4,20},{8,24},{12,28},{16,0},{20,4},{24,8},{28,12},{1,17},{... | collective-permute-start | bytes 393224 | tf_op jit(solution)/shard_map/ppermute | solution.py:13
  56.6 1.0 %copy-start.5 = (bf16[2,256,256]{2,1,0:T(8,128)(2,1)S(1)}, bf16[2,256,256]{2,1,0:T(8,128)(2,1)}, u32[]{:S(2)}) copy-start(bf16[2,256,256]{2,1,0:T(8,128)(2,1)} %copy-done.4) | copy-start | bytes 786436
  56.6 0.9 %copy-start.11 = (pred[2]{0:T(512)(128)(4,1)S(1)}, pred[2]{0:T(512)(128)(4,1)}, u32[]{:S(2)}) copy-start(pred[2]{0:T(512)(128)(4,1)} %get-tuple-element.8) | copy-start | bytes 10
  57.6 1.9 %copy-start.3 = (bf16[2,3,512,512]{3,2,1,0:T(8,128)(2,1)S(1)}, bf16[2,3,512,512]{3,2,1,0:T(8,128)(2,1)}, u32[]{:S(2)}) copy-start(bf16[2,3,512,512]{3,2,1,0:T(8,128)(2,1)} %param.14) | copy-start | bytes 9437188
where the time goes:
time: 62.6 us; the launch traced here: 62.1 us
  local copies, waits for them, and re-layouts  17.3 us (28%)
  starting transfers between devices  16.6 us (27%)
  waiting for transfers between devices  11.3 us (18%)
  matrix products  10.5 us (17%)
  other arithmetic  5.8 us (9%)
    ppermute x5, starting transfers between devices, from_partner(): lax.ppermute(value, axis, [(i, i ^ 1 << stride) for i in range(lax.axis_s...  12.7 us
    ppermute x5, waiting for transfers between devices, from_partner(): lax.ppermute(value, axis, [(i, i ^ 1 << stride) for i in range(lax.axis_s...  11.3 us
    gather x6, local copies, waits for them, and re-layouts, couple(): mats = jnp.take(pool_level, picks, axis=0)  9.54 us
    unnamed x34, local copies, waits for them, and re-layouts  3.08 us
    squeeze x1, local copies, waits for them, and re-layouts, on_device(): coupling_pool[level]  2.66 us
    ppermute x1, starting transfers between devices, extended_2(): lax.ppermute(lax.slice_in_dim(block, block.shape[dim] - width, None, axis...  2.61 us
    dot_general x5, matrix products, lift_pairs(): jnp.einsum('sr,ksp->krp', trans_level[0], pairs[:, 0], preferred_element_...  1.95 us
    gather x6, other arithmetic  1.79 us
  transfers between devices with their start and end apart: 7, of which 4 were waited for; matrix products, arithmetic and copies ran while one was open for 33% of the time, Pallas kernels for 0%

commit v1 on v0

v1 whole, which is shorter than its diff:
```python
import functools

import jax
import jax.numpy as jnp
from jax import lax
from jax.experimental import pallas as pl
from jax.experimental.pallas import tpu as pltpu
from jax.sharding import PartitionSpec as P

half_root = 0.7071067811865476
LANES = 128
ROWS = 8
NN = (((1,), (0,)), ((), ()))
NT = (((1,), (1,)), ((), ()))
TN = (((0,), (0,)), ((), ()))


def dot(a, b, dims):
    return lax.dot_general(a, b, dims, preferred_element_type=jnp.float32)


def pack(value, count):
    rows, rank = value.shape
    parts = [
        value[:, at : at + LANES].reshape(count, rows // count, LANES)
        for at in range(0, rank, LANES)
    ]
    return jnp.concatenate(parts, axis=1).astype(jnp.bfloat16)


def unpack(value, rank):
    count, rows, _ = value.shape
    k = rows * LANES // rank
    value = value.astype(jnp.float32)
    parts = [value[:, at : at + k].reshape(count * k, LANES) for at in range(0, rows, k)]
    return jnp.concatenate(parts, axis=1)


def swap_pairs(value, k):
    rows, rank = value.shape
    blocks = [value[at : at + k] for at in range(0, rows, k)]
    return jnp.concatenate([blocks[b ^ 1] for b in range(rows // k)], axis=0)


def every_other(value, k, first):
    rows, _ = value.shape
    return jnp.concatenate([value[at : at + k] for at in range(first * k, rows, 2 * k)], axis=0)


def interleave(even, odd, k):
    rows, _ = even.shape
    blocks = []
    for at in range(0, rows, k):
        blocks += [even[at : at + k], odd[at : at + k]]
    return jnp.concatenate(blocks, axis=0)


def kernel(
    n_wide, n_narrow, group, extra,
    ids, mask, probes, basis, transfer, pool, near, out,
    xv, bv, tv, p_own, pv, nv, halo, acc, coef, loc, send1, recv1, send2, recv2, outer_send, outer_recv,
    load_sem, pair_sem, halo_send, halo_recv, outer_sems,
):
    n = n_wide * n_narrow
    leaf_dev, leaf_rows, rank = bv.shape
    width = xv.shape[1]
    k = width // group
    choices = pv.shape[1]
    local_bits = leaf_dev.bit_length() - 1
    group_bits = group.bit_length() - 1
    levels = local_bits + group_bits + extra
    leaves = leaf_dev * n

    me = lax.axis_index("wide") * n_narrow + lax.axis_index("narrow")
    mine = me % group
    base = me - mine

    def place(device):
        return (device // n_narrow, device % n_narrow)

    def outer_partner(e):
        stride = group << e
        return me + (1 - 2 * ((me // stride) % 2)) * stride

    def id_at(level, node):
        return ids[2 * leaves - 2 * (leaves >> level) + node]

    loads = {}

    def load(name, src, dst):
        copy = pltpu.make_async_copy(src, dst, load_sem.at[len(loads)])
        copy.start()
        loads[name] = copy

    for i in range(leaf_dev):
        panel = pl.ds(i * leaf_rows, leaf_rows)
        load(("x", i), probes.at[panel], xv.at[panel])
        load(("b", i), basis.at[i], bv.at[i])
    low = pl.ds(0, local_bits)
    high_t = pl.ds(local_bits, levels - 1 - local_bits)
    high_p = pl.ds(local_bits, levels - local_bits)
    load("t_low", transfer.at[low], tv.at[low])
    load("t_high", transfer.at[high_t], tv.at[high_t])
    load("p_high", pool.at[high_p], pv.at[high_p])
    load("p_low", pool.at[low], p_own)
    for i in range(leaf_dev):
        load(("n", i), near.at[i], nv.at[i])

    barrier = pltpu.get_barrier_semaphore()

    def greet(device):
        pl.semaphore_signal(
            barrier, inc=1, device_id=place(device), device_id_type=pl.DeviceIdType.MESH
        )

    for s in range(1, group):
        greet(base + (mine + s) % group)
    expected = group - 1
    if extra:
        for e in range(extra):
            greet(outer_partner(e))
        up = jnp.logical_and(mine == group - 1, me < n - 1)
        down = jnp.logical_and(mine == 0, me > 0)
        pl.when(up)(lambda: greet(me + 1))
        pl.when(down)(lambda: greet(me - 1))
        expected = expected + extra + jnp.where(up, 1, 0) + jnp.where(down, 1, 0)

    def panel_of(i):
        return xv[i * leaf_rows : (i + 1) * leaf_rows, :]

    current = []
    for i in range(leaf_dev):
        loads["x", i].wait()
        loads["b", i].wait()
        current.append(dot(panel_of(i), bv[i], TN).astype(jnp.bfloat16))
    loads["t_low"].wait()
    at = 0
    starts = []
    for level in range(local_bits):
        starts.append(at)
        for value in current:
            coef[at] = value
            at += 1
        lifted = [
            (dot(current[2 * a], tv[level, 0], NN) + dot(current[2 * a + 1], tv[level, 1], NN))
            * half_root
            for a in range(len(current) // 2)
        ]
        current = [value.astype(jnp.bfloat16) for value in lifted]
    send1[...] = pack(lifted[0], group)
    recv1[pl.ds(mine, 1)] = send1[pl.ds(mine, 1)]

    pl.semaphore_wait(barrier, expected)

    def spread(send, recv, sems):
        for s in range(1, group):
            to = (mine + s) % group
            pltpu.make_async_remote_copy(
                src_ref=send.at[to],
                dst_ref=recv.at[mine],
                send_sem=pair_sem.at[sems],
                recv_sem=pair_sem.at[sems + 1],
                device_id=place(base + to),
                device_id_type=pl.DeviceIdType.MESH,
            ).start()

    def settle(ref, sem):
        most = ref.at[pl.ds(0, group - 1)]
        pltpu.make_async_copy(most, most, pair_sem.at[sem]).wait()

    spread(send1, recv1, 0)

    def halo_copy(side):
        first = (leaf_dev - 1) * leaf_rows if side == 0 else 0
        return pltpu.make_async_remote_copy(
            src_ref=xv.at[pl.ds(first, leaf_rows)],
            dst_ref=halo.at[side],
            send_sem=halo_send.at[side],
            recv_sem=halo_recv.at[side],
            device_id=place(me + 1 if side == 0 else me - 1),
            device_id_type=pl.DeviceIdType.MESH,
        )

    not_last = me < n - 1
    not_first = me > 0
    pl.when(not_last)(lambda: halo_copy(0).start())
    pl.when(not_first)(lambda: halo_copy(1).start())

    @pl.when(me == 0)
    def _():
        halo[0] = jnp.zeros_like(halo[0])

    @pl.when(me == n - 1)
    def _():
        halo[1] = jnp.zeros_like(halo[1])

    loads["p_low"].wait()
    for level in range(local_bits):
        count = leaf_dev >> level
        for a in range(count):
            matrix = p_own[level, id_at(level, me * count + a)]
            loc[starts[level] + a] = dot(coef[starts[level] + (a ^ 1)], matrix, NT)
    for i in range(leaf_dev):
        loads["n", i].wait()
        total = dot(nv[i, 1], panel_of(i), NN)
        if i > 0:
            total += dot(nv[i, 0], panel_of(i - 1), NN) * mask[i, 0].astype(jnp.float32)
        if i < leaf_dev - 1:
            total += dot(nv[i, 2], panel_of(i + 1), NN) * mask[i, 1].astype(jnp.float32)
        acc[i * leaf_rows : (i + 1) * leaf_rows, :] = total
    loads["t_high"].wait()
    loads["p_high"].wait()

    settle(recv1, 1)

    def coupled(value, level, first, count):
        chosen = jnp.concatenate(
            [jnp.full((k, rank), id_at(level, first + (b ^ 1)), jnp.int32) for b in range(count)],
            axis=0,
        )
        total = None
        for q in range(choices):
            part = jnp.where(chosen == q, value, 0.0).astype(jnp.bfloat16)
            part = dot(part, pv[level, q], NT)
            total = part if total is None else total + part
        return swap_pairs(total, k)

    value = unpack(recv1[...], rank)
    couplings = []
    for j in range(group_bits):
        level = local_bits + j
        count = group >> j
        couplings.append(coupled(value, level, base >> j, count))
        if level < levels - 1:
            left = every_other(value, k, 0).astype(jnp.bfloat16)
            right = every_other(value, k, 1).astype(jnp.bfloat16)
            value = (dot(left, tv[level, 0], NN) + dot(right, tv[level, 1], NN)) * half_root
            value = value.astype(jnp.bfloat16).astype(jnp.float32)
    outer = []
    for e in range(extra):
        level = local_bits + group_bits + e
        bit = (me // (group << e)) % 2
        outer_send[e] = pack(value, 1)[0]
        copy = pltpu.make_async_remote_copy(
            src_ref=outer_send.at[e],
            dst_ref=outer_recv.at[e],
            send_sem=outer_sems.at[0, e],
            recv_sem=outer_sems.at[1, e],
            device_id=place(outer_partner(e)),
            device_id_type=pl.DeviceIdType.MESH,
        )
        copy.start()
        copy.wait()
        other = unpack(outer_recv[e][None], rank)
        matrix = pv[level, id_at(level, me // (group << e))]
        outer.append(dot(other.astype(jnp.bfloat16), matrix, NT))
        if level < levels - 1:
            own = dot(value.astype(jnp.bfloat16), tv[level, bit], NN)
            value = (own + dot(other.astype(jnp.bfloat16), tv[level, 1 - bit], NN)) * half_root
            value = value.astype(jnp.bfloat16).astype(jnp.float32)

    field = None
    for e in reversed(range(extra)):
        level = local_bits + group_bits + e
        bit = (me // (group << e)) % 2
        below = outer[e]
        if field is not None:
            below += dot(field.astype(jnp.bfloat16), tv[level, bit], NT)
        field = below
    for j in reversed(range(group_bits)):
        level = local_bits + j
        below = couplings[j]
        if field is not None:
            coarse = field.astype(jnp.bfloat16)
            below += interleave(dot(coarse, tv[level, 0], NT), dot(coarse, tv[level, 1], NT), k)
        field = below
    send2[...] = pack(field, group)
    recv2[pl.ds(mine, 1)] = send2[pl.ds(mine, 1)]
    spread(send2, recv2, 2)

    pl.when(not_first)(lambda: halo_copy(0).wait_recv())
    first = pl.ds(0, leaf_rows)
    acc[first, :] += dot(nv[0, 0], halo[0], NN) * mask[0, 0].astype(jnp.float32)
    pl.when(not_last)(lambda: halo_copy(1).wait_recv())
    last = pl.ds((leaf_dev - 1) * leaf_rows, leaf_rows)
    acc[last, :] += dot(nv[leaf_dev - 1, 2], halo[1], NN) * mask[leaf_dev - 1, 1].astype(
        jnp.float32
    )

    settle(recv2, 3)
    fields = [unpack(recv2[...], rank).astype(jnp.bfloat16)]
    for level in reversed(range(local_bits)):
        fields = [
            (loc[starts[level] + a] + dot(fields[a // 2], tv[level, a % 2], NT)).astype(
                jnp.bfloat16
            )
            for a in range(leaf_dev >> level)
        ]
    for i in range(leaf_dev):
        rows = pl.ds(i * leaf_rows, leaf_rows)
        out[rows, :] = (acc[rows, :] + dot(bv[i], fields[i], NT)).astype(out.dtype)

    settle(send1, 0)
    settle(send2, 2)
    pl.when(not_last)(lambda: halo_copy(0).wait_send())
    pl.when(not_first)(lambda: halo_copy(1).wait_send())


def on_device(probes, leaf_basis, transfer, coupling_pool, coupling_ids, near_blocks, near_mask):
    leaf_dev, leaf_rows, rank = leaf_basis.shape
    width = probes.shape[1]
    n_narrow = lax.axis_size("narrow")
    n_wide = lax.axis_size("wide")
    n = n_narrow * n_wide
    group = min(n, width // ROWS)
    extra = (n // group).bit_length() - 1
    panel = (width // group) * rank // LANES
    bf16, f32 = jnp.bfloat16, jnp.float32
    anywhere = pl.BlockSpec(memory_space=pltpu.HBM)
    scalars = pl.BlockSpec(memory_space=pltpu.SMEM)
    slots = pltpu.VMEM((group, panel, LANES), bf16)
    outer = pltpu.VMEM((max(extra, 1), panel, LANES), bf16)
    dma = pltpu.SemaphoreType.DMA
    return pl.pallas_call(
        functools.partial(kernel, n_wide, n_narrow, group, extra),
        out_shape=jax.ShapeDtypeStruct(probes.shape, bf16),
        in_specs=[scalars, scalars] + [anywhere] * 5,
        out_specs=pl.BlockSpec(memory_space=pltpu.VMEM),
        scratch_shapes=[
            pltpu.VMEM(probes.shape, bf16),
            pltpu.VMEM(leaf_basis.shape, bf16),
            pltpu.VMEM(transfer.shape, bf16),
            pltpu.VMEM((leaf_dev.bit_length() - 1,) + coupling_pool.shape[1:], bf16),
            pltpu.VMEM(coupling_pool.shape, bf16),
            pltpu.VMEM(near_blocks.shape, bf16),
            pltpu.VMEM((2, leaf_rows, width), bf16),
            pltpu.VMEM(probes.shape, f32),
            pltpu.VMEM((2 * leaf_dev - 2, width, rank), bf16),
            pltpu.VMEM((2 * leaf_dev - 2, width, rank), f32),
            slots, slots, slots, slots, outer, outer,
            dma((3 * leaf_dev + 4,)),
            dma((4,)),
            dma((2,)),
            dma((2,)),
            dma((2, max(extra, 1))),
        ],
        compiler_params=pltpu.CompilerParams(
            collective_id=0, has_side_effects=True, vmem_limit_bytes=60 * 1024 * 1024
        ),
    )(coupling_ids, near_mask, probes, leaf_basis, transfer, coupling_pool, near_blocks)


def solution(mesh):
    in_specs = (
        P(("wide", "narrow"), None),
        P(("wide", "narrow"), None, None),
        P(),
        P(),
        P(),
        P(("wide", "narrow"), None, None, None),
        P(("wide", "narrow"), None),
    )
    return jax.shard_map(
        on_device,
        mesh=mesh,
        in_specs=in_specs,
        out_specs=P(("wide", "narrow"), None),
        check_vma=False,
    )
```

time: 62.6 us -> 23.4 us (0.37)
  Pallas kernels: 0 us -> 21.3 us
  starting transfers between devices: 16.6 us -> 0 us
  local copies, waits for them, and re-layouts: 17.3 us -> 1.87 us
  waiting for transfers between devices: 11.3 us -> 0 us
  matrix products: 10.5 us -> 0 us
  other arithmetic: 5.8 us -> 0 us
    pallas_call x0 -> x1, Pallas kernels: none -> 21.3 us  [on_device(): pl.pallas_call(functools.partial(kernel, n_wide, n_narrow, group, extra),...]
    ppermute x7 -> x0, starting transfers between devices: 16.6 us -> none  [the longest x5 12.7 us: from_partner(): lax.ppermute(value, axis, [(i, i ^ 1 << stride) for i in range(lax.axis_s...]
    ppermute x7 -> x0, waiting for transfers between devices: 11.3 us -> none  [the longest x5 11.3 us: from_partner(): lax.ppermute(value, axis, [(i, i ^ 1 << stride) for i in range(lax.axis_s...]
    dot_general x31 -> x0, matrix products: 10.5 us -> none  [the longest x5 1.95 us: lift_pairs(): jnp.einsum('sr,ksp->krp', trans_level[0], pairs[:, 0], preferred_element_...]
    gather x6 -> x0, local copies, waits for them, and re-layouts: 9.54 us -> none  [couple(): mats = jnp.take(pool_level, picks, axis=0)]
    squeeze x1 -> x0, local copies, waits for them, and re-layouts: 2.66 us -> none  [on_device(): coupling_pool[level]]
    gather x6 -> x0, other arithmetic: 1.79 us -> none
    unnamed x34 -> x1, local copies, waits for them, and re-layouts: 3.08 us -> 1.87 us
  transfers between devices with their start and end apart: 7 -> 0, of which waited for: 4 -> 0; matrix products, arithmetic and copies ran while one was open for 33% -> 0% of each run, Pallas kernels for 0% -> 0%
where the time goes in v1:
time: 23.4 us; the launch traced here: 23.2 us
  Pallas kernels  21.3 us (91%)
  local copies, waits for them, and re-layouts  1.87 us (8%)
    pallas_call x1, Pallas kernels, on_device(): pl.pallas_call(functools.partial(kernel, n_wide, n_narrow, group, extra),...  21.3 us
    unnamed x1, local copies, waits for them, and re-layouts  1.87 us

profile of v1, /device:TPU:0, one launch (start us, length us, event | category | flops | bytes accessed | tf_op | source)
XLA Modules:
  0.0 23.2 jit_solution(8362549559648930652)
XLA Ops:
  0.0 21.3 %shard_map.73 = bf16[1024,256]{1,0:T(8,128)(2,1)} custom-call(s32[126]{0:T(128)} %ids.1, s32[2,2]{1,0:T(2,128)} %mask.1, bf16[1024,256]{1,0:T(8,128)(2,1)} %probes.1, bf16[2,512,256]{2,1,0:T(8,128)(2,1)} %basis.1, bf16[5,2,256,256]{3,2,1,0:T(8,128)(2,1)} %transfer.1, bf16[6,3,256,256]{3,2,1,0:T(8,128)(2,1)} %pool.1, bf16[2,3,512,512]{3,2,1,0:T(8,128)(2,1)} %near.1), custom_call_target="tpu_custom_call" | custom-call | tf_op jit(solution)/shard_map/pallas_call | solution.py:324
  21.3 1.9 %copy.9 = bf16[1024,256]{1,0:T(8,128)(2,1)} copy(bf16[1024,256]{1,0:T(8,128)(2,1)} %shard_map.73) | data formatting | bytes 1048576

commit v2 on v1

--- a/solution.py
+++ b/solution.py
@@ -57,8 +57,8 @@
 
 def kernel(
     n_wide, n_narrow, group, extra,
-    ids, mask, probes, basis, transfer, pool, near, out,
-    xv, bv, tv, p_own, pv, nv, halo, acc, coef, loc, send1, recv1, send2, recv2, outer_send, outer_recv,
+    ids_hbm, mask_hbm, probes, basis, transfer, pool, near, out,
+    ids, mask, xv, bv, tv, p_own, pv, nv, halo, acc, coef, loc, send1, recv1, send2, recv2, outer_send, outer_recv,
     load_sem, pair_sem, halo_send, halo_recv, outer_sems,
 ):
     n = n_wide * n_narrow
@@ -100,6 +100,8 @@
     high_t = pl.ds(local_bits, levels - 1 - local_bits)
     high_p = pl.ds(local_bits, levels - local_bits)
     load("t_low", transfer.at[low], tv.at[low])
+    load("ids", ids_hbm, ids)
+    load("mask", mask_hbm, mask)
     load("t_high", transfer.at[high_t], tv.at[high_t])
     load("p_high", pool.at[high_p], pv.at[high_p])
     load("p_low", pool.at[low], p_own)
@@ -195,6 +197,8 @@
         halo[1] = jnp.zeros_like(halo[1])
 
     loads["p_low"].wait()
+    loads["ids"].wait()
+    loads["mask"].wait()
     for level in range(local_bits):
         count = leaf_dev >> level
         for a in range(count):
@@ -316,17 +320,21 @@
     extra = (n // group).bit_length() - 1
     panel = (width // group) * rank // LANES
     bf16, f32 = jnp.bfloat16, jnp.float32
+    arrays = (
+        coupling_ids, near_mask, probes, leaf_basis, transfer, coupling_pool, near_blocks,
+    )
     anywhere = pl.BlockSpec(memory_space=pltpu.HBM)
-    scalars = pl.BlockSpec(memory_space=pltpu.SMEM)
     slots = pltpu.VMEM((group, panel, LANES), bf16)
     outer = pltpu.VMEM((max(extra, 1), panel, LANES), bf16)
     dma = pltpu.SemaphoreType.DMA
     return pl.pallas_call(
         functools.partial(kernel, n_wide, n_narrow, group, extra),
-        out_shape=jax.ShapeDtypeStruct(probes.shape, bf16),
-        in_specs=[scalars, scalars] + [anywhere] * 5,
+        out_shape=pltpu.VMEM(probes.shape, bf16),
+        in_specs=[anywhere] * 7,
         out_specs=pl.BlockSpec(memory_space=pltpu.VMEM),
         scratch_shapes=[
+            pltpu.SMEM(coupling_ids.shape, jnp.int32),
+            pltpu.SMEM(near_mask.shape, jnp.int32),
             pltpu.VMEM(probes.shape, bf16),
             pltpu.VMEM(leaf_basis.shape, bf16),
             pltpu.VMEM(transfer.shape, bf16),
@@ -338,16 +346,16 @@
             pltpu.VMEM((2 * leaf_dev - 2, width, rank), bf16),
             pltpu.VMEM((2 * leaf_dev - 2, width, rank), f32),
             slots, slots, slots, slots, outer, outer,
-            dma((3 * leaf_dev + 4,)),
+            dma((3 * leaf_dev + 6,)),
             dma((4,)),
             dma((2,)),
             dma((2,)),
             dma((2, max(extra, 1))),
         ],
         compiler_params=pltpu.CompilerParams(
-            collective_id=0, has_side_effects=True, vmem_limit_bytes=60 * 1024 * 1024
+            collective_id=0, has_side_effects=True, vmem_limit_bytes=32 * 1024 * 1024
         ),
-    )(coupling_ids, near_mask, probes, leaf_basis, transfer, coupling_pool, near_blocks)
+    )(*[pltpu.with_memory_space_constraint(array, pltpu.HBM) for array in arrays])
 
 
 def solution(mesh):

time: 23.4 us -> 20.8 us (0.89)
  Pallas kernels: 21.3 us -> 19.8 us
  local copies, waits for them, and re-layouts: 1.87 us -> 0.8 us
    pallas_call x1, Pallas kernels: 21.3 us -> 19.8 us  [on_device(): pl.pallas_call(functools.partial(kernel, n_wide, n_narrow, group, extra),...]
    unnamed x1, local copies, waits for them, and re-layouts: 1.87 us -> 0.8 us
where the time goes in v2:
time: 20.8 us; the launch traced here: 20.6 us
  Pallas kernels  19.8 us (95%)
  local copies, waits for them, and re-layouts  0.8 us (4%)
    pallas_call x1, Pallas kernels, on_device(): pl.pallas_call(functools.partial(kernel, n_wide, n_narrow, group, extra),...  19.8 us
    unnamed x1, local copies, waits for them, and re-layouts  0.8 us

profile of v2, /device:TPU:0, one launch (start us, length us, event | category | flops | bytes accessed | tf_op | source)
XLA Modules:
  0.0 20.6 jit_solution(11913042597741319658)
XLA Ops:
  0.0 19.8 %shard_map.73 = bf16[1024,256]{1,0:T(8,128)(2,1)S(1)} custom-call(s32[126]{0:T(128)} %ids_hbm.1, s32[2,2]{1,0:T(2,128)} %mask_hbm.1, bf16[1024,256]{1,0:T(8,128)(2,1)} %probes.1, bf16[2,512,256]{2,1,0:T(8,128)(2,1)} %basis.1, bf16[5,2,256,256]{3,2,1,0:T(8,128)(2,1)} %transfer.1, bf16[6,3,256,256]{3,2,1,0:T(8,128)(2,1)} %pool.1, bf16[2,3,512,512]{3,2,1,0:T(8,128)(2,1)} %near.1), custom_call_target="tpu_custom_call" | custom-call | tf_op jit(solution)/shard_map/pallas_call | solution.py:330
  19.8 0.8 %copy.9 = bf16[1024,256]{1,0:T(8,128)(2,1)} copy(bf16[1024,256]{1,0:T(8,128)(2,1)S(1)} %shard_map.73) | data formatting | bytes 1048576

commit v3 on v2

--- a/solution.py
+++ b/solution.py
@@ -71,12 +71,34 @@
     levels = local_bits + group_bits + extra
     leaves = leaf_dev * n
 
-    me = lax.axis_index("wide") * n_narrow + lax.axis_index("narrow")
-    mine = me % group
-    base = me - mine
+    wide, narrow = lax.axis_index("wide"), lax.axis_index("narrow")
+    me = wide * n_narrow + narrow
+    group_wide = group // n_narrow
+    wide_base = wide // group_wide * group_wide if extra else 0
+    base = wide_base * n_narrow
+    mine = me - base
 
     def place(device):
         return (device // n_narrow, device % n_narrow)
+
+    def turned(position, step, count):
+        moved = position + step
+        return jnp.where(moved >= count, moved - count, moved) if step else position
+
+    turns_narrow = []
+    for step in range(n_narrow):
+        moved = narrow + step
+        carried = moved >= n_narrow
+        turns_narrow.append((jnp.where(carried, moved - n_narrow, moved), carried))
+    turns_wide = [
+        turned(wide - wide_base, step % group_wide, group_wide) for step in range(group_wide + 1)
+    ]
+    others = []
+    for step in range(1, group):
+        to_narrow, carried = turns_narrow[step % n_narrow]
+        at = step // n_narrow
+        to_wide = jnp.where(carried, turns_wide[at + 1], turns_wide[at])
+        others.append((wide_base + to_wide, to_narrow, to_wide * n_narrow + to_narrow))
 
     def outer_partner(e):
         stride = group << e
@@ -110,21 +132,21 @@
 
     barrier = pltpu.get_barrier_semaphore()
 
-    def greet(device):
+    def greet(device_id):
         pl.semaphore_signal(
-            barrier, inc=1, device_id=place(device), device_id_type=pl.DeviceIdType.MESH
+            barrier, inc=1, device_id=device_id, device_id_type=pl.DeviceIdType.MESH
         )
 
-    for s in range(1, group):
-        greet(base + (mine + s) % group)
+    for to_wide, to_narrow, _ in others:
+        greet((to_wide, to_narrow))
     expected = group - 1
     if extra:
         for e in range(extra):
-            greet(outer_partner(e))
+            greet(place(outer_partner(e)))
         up = jnp.logical_and(mine == group - 1, me < n - 1)
         down = jnp.logical_and(mine == 0, me > 0)
-        pl.when(up)(lambda: greet(me + 1))
-        pl.when(down)(lambda: greet(me - 1))
+        pl.when(up)(lambda: greet(place(me + 1)))
+        pl.when(down)(lambda: greet(place(me - 1)))
         expected = expected + extra + jnp.where(up, 1, 0) + jnp.where(down, 1, 0)
 
     def panel_of(i):
@@ -152,17 +174,32 @@
     send1[...] = pack(lifted[0], group)
     recv1[pl.ds(mine, 1)] = send1[pl.ds(mine, 1)]
 
+    loads["p_low"].wait()
+    loads["ids"].wait()
+    loads["mask"].wait()
+    for level in range(local_bits):
+        count = leaf_dev >> level
+        for a in range(count):
+            matrix = p_own[level, id_at(level, me * count + a)]
+            loc[starts[level] + a] = dot(coef[starts[level] + (a ^ 1)], matrix, NT)
+    for i in range(leaf_dev):
+        loads["n", i].wait()
+        total = dot(nv[i, 1], panel_of(i), NN)
+        if i > 0:
+            total += dot(nv[i, 0], panel_of(i - 1), NN) * mask[i, 0].astype(jnp.float32)
+        if i < leaf_dev - 1:
+            total += dot(nv[i, 2], panel_of(i + 1), NN) * mask[i, 1].astype(jnp.float32)
+        acc[i * leaf_rows : (i + 1) * leaf_rows, :] = total
     pl.semaphore_wait(barrier, expected)
 
     def spread(send, recv, sems):
-        for s in range(1, group):
-            to = (mine + s) % group
+        for to_wide, to_narrow, to in others:
             pltpu.make_async_remote_copy(
                 src_ref=send.at[to],
                 dst_ref=recv.at[mine],
                 send_sem=pair_sem.at[sems],
                 recv_sem=pair_sem.at[sems + 1],
-                device_id=place(base + to),
+                device_id=(to_wide, to_narrow),
                 device_id_type=pl.DeviceIdType.MESH,
             ).start()
 
@@ -196,22 +233,6 @@
     def _():
         halo[1] = jnp.zeros_like(halo[1])
 
-    loads["p_low"].wait()
-    loads["ids"].wait()
-    loads["mask"].wait()
-    for level in range(local_bits):
-        count = leaf_dev >> level
-        for a in range(count):
-            matrix = p_own[level, id_at(level, me * count + a)]
-            loc[starts[level] + a] = dot(coef[starts[level] + (a ^ 1)], matrix, NT)
-    for i in range(leaf_dev):
-        loads["n", i].wait()
-        total = dot(nv[i, 1], panel_of(i), NN)
-        if i > 0:
-            total += dot(nv[i, 0], panel_of(i - 1), NN) * mask[i, 0].astype(jnp.float32)
-        if i < leaf_dev - 1:
-            total += dot(nv[i, 2], panel_of(i + 1), NN) * mask[i, 1].astype(jnp.float32)
-        acc[i * leaf_rows : (i + 1) * leaf_rows, :] = total
     loads["t_high"].wait()
     loads["p_high"].wait()
 

time: 20.8 us -> 20.6 us (level)
  no operation moved by 1% of the time
where the time goes in v3:
time: 20.6 us; the launch traced here: 20.5 us
  Pallas kernels  19.7 us (96%)
  local copies, waits for them, and re-layouts  0.8 us (4%)
    pallas_call x1, Pallas kernels, on_device(): pl.pallas_call(functools.partial(kernel, n_wide, n_narrow, group, extra),...  19.7 us
    unnamed x1, local copies, waits for them, and re-layouts  0.8 us

profile of v3, /device:TPU:0, one launch (start us, length us, event | category | flops | bytes accessed | tf_op | source)
XLA Modules:
  0.0 20.5 jit_solution(5129968841882719440)
XLA Ops:
  0.0 19.7 %shard_map.73 = bf16[1024,256]{1,0:T(8,128)(2,1)S(1)} custom-call(s32[126]{0:T(128)} %ids_hbm.1, s32[2,2]{1,0:T(2,128)} %mask_hbm.1, bf16[1024,256]{1,0:T(8,128)(2,1)} %probes.1, bf16[2,512,256]{2,1,0:T(8,128)(2,1)} %basis.1, bf16[5,2,256,256]{3,2,1,0:T(8,128)(2,1)} %transfer.1, bf16[6,3,256,256]{3,2,1,0:T(8,128)(2,1)} %pool.1, bf16[2,3,512,512]{3,2,1,0:T(8,128)(2,1)} %near.1), custom_call_target="tpu_custom_call" | custom-call | tf_op jit(solution)/shard_map/pallas_call | solution.py:351
  19.7 0.8 %copy.9 = bf16[1024,256]{1,0:T(8,128)(2,1)} copy(bf16[1024,256]{1,0:T(8,128)(2,1)S(1)} %shard_map.73) | data formatting | bytes 1048576

commit v4 on v3

--- a/solution.py
+++ b/solution.py
@@ -58,7 +58,7 @@
 def kernel(
     n_wide, n_narrow, group, extra,
     ids_hbm, mask_hbm, probes, basis, transfer, pool, near, out,
-    ids, mask, xv, bv, tv, p_own, pv, nv, halo, acc, coef, loc, send1, recv1, send2, recv2, outer_send, outer_recv,
+    ids, mask, xv, bv, tv, p_own, pv, nv, halo, acc, joined, coef, loc, send1, recv1, send2, recv2, outer_send, outer_recv,
     load_sem, pair_sem, halo_send, halo_recv, outer_sems,
 ):
     n = n_wide * n_narrow
@@ -312,9 +312,15 @@
         jnp.float32
     )
 
+    for i in range(leaf_dev):
+        rows = pl.ds(i * leaf_rows, leaf_rows)
+        own = loc[starts[0] + i].astype(jnp.bfloat16)
+        acc[rows, :] += dot(bv[i], own, NT)
+        joined[i] = dot(bv[i], tv[0, i % 2], NN).astype(jnp.bfloat16)
+
     settle(recv2, 3)
     fields = [unpack(recv2[...], rank).astype(jnp.bfloat16)]
-    for level in reversed(range(local_bits)):
+    for level in reversed(range(1, local_bits)):
         fields = [
             (loc[starts[level] + a] + dot(fields[a // 2], tv[level, a % 2], NT)).astype(
                 jnp.bfloat16
@@ -323,7 +329,7 @@
         ]
     for i in range(leaf_dev):
         rows = pl.ds(i * leaf_rows, leaf_rows)
-        out[rows, :] = (acc[rows, :] + dot(bv[i], fields[i], NT)).astype(out.dtype)
+        out[rows, :] = (acc[rows, :] + dot(joined[i], fields[i // 2], NT)).astype(out.dtype)
 
     settle(send1, 0)
     settle(send2, 2)
@@ -364,6 +370,7 @@
             pltpu.VMEM(near_blocks.shape, bf16),
             pltpu.VMEM((2, leaf_rows, width), bf16),
             pltpu.VMEM(probes.shape, f32),
+            pltpu.VMEM(leaf_basis.shape, bf16),
             pltpu.VMEM((2 * leaf_dev - 2, width, rank), bf16),
             pltpu.VMEM((2 * leaf_dev - 2, width, rank), f32),
             slots, slots, slots, slots, outer, outer,

time: 20.6 us -> 20.4 us (level)
  no operation moved by 1% of the time
where the time goes in v4:
time: 20.4 us; the launch traced here: 20.3 us
  Pallas kernels  19.5 us (96%)
  local copies, waits for them, and re-layouts  0.8 us (4%)
    pallas_call x1, Pallas kernels, on_device(): pl.pallas_call(functools.partial(kernel, n_wide, n_narrow, group, extra),...  19.5 us
    unnamed x1, local copies, waits for them, and re-layouts  0.8 us

profile of v4, /device:TPU:0, one launch (start us, length us, event | category | flops | bytes accessed | tf_op | source)
XLA Modules:
  0.0 20.3 jit_solution(16210413521599226583)
XLA Ops:
  0.0 19.5 %shard_map.73 = bf16[1024,256]{1,0:T(8,128)(2,1)S(1)} custom-call(s32[126]{0:T(128)} %ids_hbm.1, s32[2,2]{1,0:T(2,128)} %mask_hbm.1, bf16[1024,256]{1,0:T(8,128)(2,1)} %probes.1, bf16[2,512,256]{2,1,0:T(8,128)(2,1)} %basis.1, bf16[5,2,256,256]{3,2,1,0:T(8,128)(2,1)} %transfer.1, bf16[6,3,256,256]{3,2,1,0:T(8,128)(2,1)} %pool.1, bf16[2,3,512,512]{3,2,1,0:T(8,128)(2,1)} %near.1), custom_call_target="tpu_custom_call" | custom-call | tf_op jit(solution)/shard_map/pallas_call | solution.py:357
  19.5 0.8 %copy.9 = bf16[1024,256]{1,0:T(8,128)(2,1)} copy(bf16[1024,256]{1,0:T(8,128)(2,1)S(1)} %shard_map.73) | data formatting | bytes 1048576
